TPU v7x, 128 devices: a whole 4x4x4 slice. The times are simulated.
128 devices in a mesh: pipe: 4 (over y_lo, core), expert: 32 (over x, z, y_hi).
Axes of the slice: x: 4, y: 4 (y_hi: 2, y_lo: 2; y = y_hi * 2 + y_lo), z: 4, core: 2. Of those that a mesh axis runs over, the one named last changes fastest.
Arguments:
- next_input: bfloat16 [4, 8192, 2048], P('pipe', 'expert'), may hold values from -6 to 6
- prev_input: bfloat16 [4, 8192, 2048], P('pipe', 'expert'), may hold values from -6 to 6
- next_cot: bfloat16 [4, 8192, 2048], P('pipe', 'expert'), may hold values from -6 to 6
- gate_weight: bfloat16 [4, 32, 2048, 768], P('pipe', 'expert'), may hold values from -0.125 to 0.125
- up_weight: bfloat16 [4, 32, 2048, 768], P('pipe', 'expert'), may hold values from -0.125 to 0.125
- down_weight: bfloat16 [4, 32, 768, 2048], P('pipe', 'expert'), may hold values from -0.21875 to 0.21875
- router: bfloat16 [4, 2048, 32], P('pipe'), may hold values from -0.125 to 0.125
- gain: float32 [4, 2048], P('pipe'), may hold values from 0.1 to 1.9
- next_routes: int32 [4, 8192, 2], P('pipe', 'expert'), may hold values from 0 to 31, all different within a row
- prev_routes: int32 [4, 8192, 2], P('pipe', 'expert'), may hold values from 0 to 31, all different within a row
- next_priority: int32 [4, 8192], P('pipe', 'expert'), may hold values from 0 to 8191, each once within a row
- prev_priority: int32 [4, 8192], P('pipe', 'expert'), may hold values from 0 to 8191, each once within a row
Outputs:
- forward_out: bfloat16 [4, 8192, 2048], P('pipe', 'expert')
- input_grad: bfloat16 [4, 8192, 2048], P('pipe', 'expert')
- gate_grad: bfloat16 [4, 32, 2048, 768], P('pipe', 'expert')
- up_grad: bfloat16 [4, 32, 2048, 768], P('pipe', 'expert')
- down_grad: bfloat16 [4, 32, 768, 2048], P('pipe', 'expert')
- router_grad: float32 [4, 2048, 32], P('pipe')
- gain_grad: float32 [4, 2048], P('pipe')
All inputs are finite; a program needn't handle non-finite values.
Results may differ from a plain program's by a relative error of at most 0.0085.
Values may be sent and summed in bfloat16 or wider, within the bound.
A program may use at most 128 MiB of HBM per device.

v0:
```python
import jax
import jax.numpy as jnp
from jax import lax
from jax.sharding import PartitionSpec as P

EPS = 1e-06


def passed_along(block, axis, distance):
    devices = range(lax.axis_size(axis))
    route = [((i - distance) % len(devices), i) for i in devices]
    return lax.ppermute(block, axis, route)


def rms_scaled(values, gain):
    scale = lax.rsqrt(jnp.mean(values * values, axis=-1, keepdims=True) + EPS)
    return values * scale * gain


def pair_weights(selected):
    lifted = jax.nn.sigmoid(selected)
    return lifted / jnp.sum(lifted, axis=-1, keepdims=True)


def slot_table(routes, priority, experts, capacity):
    top = routes.shape[1]
    picks = routes.reshape(-1)
    order = jnp.repeat(priority, top)
    same = picks[:, None] == picks[None, :]
    before = order[None, :] < order[:, None]
    rank = jnp.sum(jnp.where(same & before, 1, 0), axis=1).astype(jnp.int32)
    kept = rank < capacity
    slots = jnp.where(kept, picks * capacity + rank, experts * capacity)
    match = slots[None, :] == jnp.arange(experts * capacity, dtype=jnp.int32)[:, None]
    filled = jnp.any(match, axis=1)
    source = jnp.sum(
        jnp.where(match, jnp.arange(picks.shape[0], dtype=jnp.int32)[None, :], 0), axis=1
    )
    return (slots, filled, source)


def prepare(section_in, gain, router, routes, priority, capacity):
    experts = router.shape[-1]
    top = routes.shape[1]
    values = section_in.astype(jnp.float32)
    normed = rms_scaled(values, gain).astype(jnp.bfloat16)
    logits = jnp.dot(normed, router, preferred_element_type=jnp.float32)
    selected = jnp.take_along_axis(logits, routes, axis=1)
    slots, filled, source = slot_table(routes, priority, experts, capacity)
    token = source // top
    rows = jnp.where(filled[:, None], normed[token], jnp.zeros_like(normed[token]))
    rows = rows.reshape(experts, capacity, normed.shape[1])
    return (values, normed, selected, slots, filled, source, rows)


def pick_rows(table, slots):
    flat = table.reshape(-1, table.shape[-1])
    padded = jnp.concatenate([flat, jnp.zeros((1, flat.shape[1]), flat.dtype)], axis=0)
    return padded[slots].astype(jnp.float32)


def combine(values, selected, slots, produced):
    top = selected.shape[1]
    weights = pair_weights(selected).reshape(-1, 1)
    taken = pick_rows(produced, slots) * weights
    total = jnp.sum(taken.reshape(values.shape[0], top, values.shape[1]), axis=1)
    return (values + total).astype(jnp.bfloat16)


def expert_forward(received, gate_w, up_w, down_w):
    flat = received.reshape(-1, received.shape[-1])
    gate = jnp.dot(flat, gate_w[0], preferred_element_type=jnp.float32)
    upper = jnp.dot(flat, up_w[0], preferred_element_type=jnp.float32)
    active = (gate * jax.nn.sigmoid(gate) * upper).astype(jnp.bfloat16)
    result = jnp.dot(active, down_w[0], preferred_element_type=jnp.float32).astype(jnp.bfloat16)
    return result.reshape(received.shape)


def expert_backward(received, cot_recv, scale_recv, gate_w, up_w, down_w):
    width = received.shape[-1]
    flat = received.reshape(-1, width)
    cot = cot_recv.reshape(-1, width)
    scales = scale_recv.reshape(-1, 1)
    gate_m, up_m, down_m = (gate_w[0], up_w[0], down_w[0])
    gate = jnp.dot(flat, gate_m, preferred_element_type=jnp.float32)
    upper = jnp.dot(flat, up_m, preferred_element_type=jnp.float32)
    sig = jax.nn.sigmoid(gate)
    lifted = gate * sig
    active = (lifted * upper).astype(jnp.bfloat16)
    result = jnp.dot(active, down_m, preferred_element_type=jnp.float32).astype(jnp.bfloat16)
    inner = jnp.sum(
        cot.astype(jnp.float32) * result.astype(jnp.float32), axis=-1, keepdims=True
    ).astype(jnp.bfloat16)
    scaled = (scales.astype(jnp.float32) * cot.astype(jnp.float32)).astype(jnp.bfloat16)
    down_part = jnp.dot(active.T, scaled, preferred_element_type=jnp.float32)
    act_grad = jnp.dot(scaled, down_m.T, preferred_element_type=jnp.float32)
    gate_part = (act_grad * upper * sig * (1.0 + gate * (1.0 - sig))).astype(jnp.bfloat16)
    up_part = (act_grad * lifted).astype(jnp.bfloat16)
    gate_wgrad = jnp.dot(flat.T, gate_part, preferred_element_type=jnp.float32)
    up_wgrad = jnp.dot(flat.T, up_part, preferred_element_type=jnp.float32)
    row_grad = jnp.dot(gate_part, gate_m.T, preferred_element_type=jnp.float32)
    row_grad = (row_grad + jnp.dot(up_part, up_m.T, preferred_element_type=jnp.float32)).astype(
        jnp.bfloat16
    )
    return (
        row_grad.reshape(received.shape),
        inner.reshape(received.shape[:2] + (1,)),
        (gate_wgrad[None], up_wgrad[None], down_part[None]),
    )


def source_backward(values, normed, selected, routes, gain, router, slots, row_grad, inner, cot_in):
    top = routes.shape[1]
    experts = router.shape[-1]
    width = values.shape[1]
    pulled = pick_rows(row_grad, slots).reshape(values.shape[0], top, width)
    dnormed = jnp.sum(pulled, axis=1)
    dweight = pick_rows(inner, slots).reshape(values.shape[0], top)
    _, pull = jax.vjp(pair_weights, selected)
    dsel = pull(dweight)[0]
    onehot = (routes[:, :, None] == jnp.arange(experts, dtype=jnp.int32)[None, None, :]).astype(
        jnp.float32
    )
    dlogits = jnp.sum(onehot * dsel[:, :, None], axis=1)
    router_f = router.astype(jnp.float32)
    dnormed = dnormed + jnp.dot(dlogits, router_f.T, precision=lax.Precision.HIGHEST)
    router_part = jnp.dot(normed.astype(jnp.float32).T, dlogits, precision=lax.Precision.HIGHEST)
    _, pull_norm = jax.vjp(rms_scaled, values, gain)
    dvalues, dgain = pull_norm(dnormed)
    grad_in = (cot_in.astype(jnp.float32) + dvalues).astype(jnp.bfloat16)
    return (grad_in, router_part, dgain)


def per_device(
    next_input,
    prev_input,
    next_cot,
    gate_weight,
    up_weight,
    down_weight,
    router,
    gain,
    next_routes,
    prev_routes,
    next_priority,
    prev_priority,
):
    experts = router.shape[-1]
    tokens = next_input.shape[1]
    top = next_routes.shape[-1]
    capacity = (5 * top * tokens + 4 * experts - 1) // (4 * experts)
    gate_w, up_w, down_w = (gate_weight[0], up_weight[0], down_weight[0])
    router_w, gain_v = (router[0], gain[0])
    section_in = passed_along(next_input, "pipe", 1)[0]
    cot_in = passed_along(next_cot, "pipe", -1)[0]
    fwd_values, fwd_normed, fwd_selected, fwd_slots, fwd_filled, fwd_source, fwd_rows = prepare(
        section_in, gain_v, router_w, next_routes[0], next_priority[0], capacity
    )
    routes_prev = prev_routes[0]
    values, normed, selected, slots, filled, source, rows = prepare(
        prev_input[0], gain_v, router_w, routes_prev, prev_priority[0], capacity
    )
    token = source // top
    cot_rows = jnp.where(filled[:, None], cot_in[token], jnp.zeros_like(cot_in[token])).reshape(
        rows.shape
    )
    flat_weights = pair_weights(selected).reshape(-1)
    scale_rows = (
        jnp.where(filled, flat_weights[source], 0.0)
        .astype(jnp.bfloat16)
        .reshape(rows.shape[:2] + (1,))
    )
    produced = expert_forward(
        lax.all_to_all(fwd_rows, "expert", split_axis=0, concat_axis=0, tiled=True),
        gate_w,
        up_w,
        down_w,
    )
    returned = lax.all_to_all(produced, "expert", split_axis=0, concat_axis=0, tiled=True)
    forward = combine(fwd_values, fwd_selected, fwd_slots, returned)
    row_grad, inner, weight_grads = expert_backward(
        lax.all_to_all(rows, "expert", split_axis=0, concat_axis=0, tiled=True),
        lax.all_to_all(cot_rows, "expert", split_axis=0, concat_axis=0, tiled=True),
        lax.all_to_all(scale_rows, "expert", split_axis=0, concat_axis=0, tiled=True),
        gate_w,
        up_w,
        down_w,
    )
    back_rows, back_inner, weight_grads = (
        lax.all_to_all(row_grad, "expert", split_axis=0, concat_axis=0, tiled=True),
        lax.all_to_all(inner, "expert", split_axis=0, concat_axis=0, tiled=True),
        weight_grads,
    )
    grad_in, router_part, dgain = source_backward(
        values,
        normed,
        selected,
        routes_prev,
        gain_v,
        router_w,
        slots,
        back_rows,
        back_inner,
        cot_in,
    )
    router_total, gain_total = lax.psum((router_part, dgain), "expert")
    gate_wgrad, up_wgrad, down_part = weight_grads
    return (
        forward[None],
        grad_in[None],
        gate_wgrad.astype(jnp.bfloat16)[None],
        up_wgrad.astype(jnp.bfloat16)[None],
        down_part.astype(jnp.bfloat16)[None],
        router_total[None],
        gain_total[None],
    )


def solution(mesh):
    placed = (
        P("pipe", "expert", None),
        P("pipe", "expert", None),
        P("pipe", "expert", None),
        P("pipe", "expert", None, None),
        P("pipe", "expert", None, None),
        P("pipe", "expert", None, None),
        P("pipe", None, None),
        P("pipe", None),
        P("pipe", "expert", None),
        P("pipe", "expert", None),
        P("pipe", "expert"),
        P("pipe", "expert"),
    )
    return jax.shard_map(
        per_device,
        mesh=mesh,
        in_specs=placed,
        out_specs=(
            P("pipe", "expert", None),
            P("pipe", "expert", None),
            P("pipe", "expert", None, None),
            P("pipe", "expert", None, None),
            P("pipe", "expert", None, None),
            P("pipe", None, None),
            P("pipe", None),
        ),
        check_vma=False,
    )
```

profile of v0, /device:TPU:0, one launch (start us, length us, event | category | flops | bytes accessed | tf_op | source)
XLA Modules:
  0.0 811.6 jit_solution(14537587586290588324)
XLA Ops:
  13.4 4.5 gather_fusion.8
  19.6 4.3 gather_fusion.2
  24.9 10.6 %all-to-all-start.2 = ((bf16[32,20,1]{1,2,0:T(2,128)(2,1)}), bf16[32,20,1]{1,2,0:T(2,128)(2,1)S(1)}, u32[]{:S(2)}, u32[]{:S(2)}) async-start(bf16[32,20,1]{1,2,0:T(2,128)(2,1)} %convert_element_type.225), calls=%async_computation.2 | async-start | bytes 32768 | tf_op jit(solution)/shard_map/all_to_all | solution.py:184
  38.2 8.3 %gather_fusion.4 = bf16[640,2048]{1,0:T(8,128)(2,1)} fusion(bf16[256,2048]{1,0:T(8,128)(2,1)} %fusion.27, s32[1024]{0:T(1024)S(1)} %pad_clamp_fusion.1), kind=kCustom, calls=%fused_computation.6 | custom fusion | bytes 5245440 | tf_op jit(solution)/shard_map/gather | solution.py:51
  46.5 5.1 gather.37
  51.6 8.3 %gather_fusion.3 = bf16[640,2048]{1,0:T(8,128)(2,1)} fusion(bf16[256,2048]{1,0:T(8,128)(2,1)} %bitcast.13, s32[1024]{0:T(1024)S(1)} %pad_clamp_fusion.1), kind=kCustom, calls=%fused_computation.5 | custom fusion | bytes 5245440 | tf_op jit(solution)/shard_map/gather | solution.py:164
  59.9 5.1 gather.35
  65.0 4.9 broadcast_select_fusion.1
  69.9 50.8 %all_to_all.35 = bf16[32,20,2048]{2,1,0:T(8,128)(2,1)} all-to-all(bf16[32,20,2048]{2,1,0:T(8,128)(2,1)} %get-tuple-element.22), channel_id=1, replica_groups=mesh['pipe'=4,'expert'=32] {'expert'}, dimensions={0} | all-to-all | bytes 5242880 | tf_op jit(solution)/shard_map/all_to_all | solution.py:183
  120.7 5.3 all-to-all-start.4
  126.0 4.1 multiply_convert_fusion
  130.1 5.2 convert_element_type.193
  135.3 32.4 %all-to-all-done.4 = bf16[32,20,2048]{2,1,0:T(8,128)(2,1)} async-done(((bf16[32,20,2048]{2,1,0:T(8,128)(2,1)}), bf16[32,20,2048]{2,1,0:T(8,128)(2,1)}, u32[]{:S(2)}, u32[]{:S(2)}) %all-to-all-start.4) | async-done | bytes 2621472 | tf_op jit(solution)/shard_map/all_to_all | solution.py:182
  167.7 5.2 reshape.455
  172.9 5.0 fusion.11
  180.2 4.3 multiply_convert_fusion.3
  184.5 5.5 reshape.465
  190.0 6.0 multiply_reduce_fusion
  196.8 7.2 all-to-all-start.6
  204.0 4.5 fusion.9
  208.5 3.8 add_convert_fusion
  212.3 5.1 reshape.456
  217.4 10.0 %all-to-all-start.5 = ((bf16[32,20,2048]{2,1,0:T(8,128)(2,1)}), bf16[32,20,2048]{2,1,0:T(8,128)(2,1)}, u32[]{:S(2)}, u32[]{:S(2)}) async-start(bf16[32,20,2048]{2,1,0:T(8,128)(2,1)} %reshape.456), calls=%async_computation.5 | async-start | bytes 6291456 | tf_op jit(solution)/shard_map/all_to_all | solution.py:190
  229.4 45.4 %collective-permute-done = bf16[1,256,2048]{2,1,0:T(8,128)(2,1)} collective-permute-done((bf16[1,256,2048]{2,1,0:T(8,128)(2,1)}, bf16[1,256,2048]{2,1,0:T(8,128)(2,1)}, u32[]{:S(2)}, u32[]{:S(2)}) %collective-permute-start) | collective-permute-done | bytes 1048608 | tf_op jit(solution)/shard_map/ppermute | solution.py:12
  280.5 5.2 reshape.457
  289.3 7.3 gather_fusion.5
  296.6 5.5 reshape.464
  302.1 8.5 %reduce_sum.179 = f32[256,2048]{1,0:T(8,128)} reduce(f32[256,2,2048]{2,1,0:T(2,128)} %reshape.464, f32[]{:T(128)} %constant.59.clone.1), dimensions={1}, to_apply=%region_11.13 | reduce | flops 524288 | bytes 6291460 | tf_op jit(solution)/shard_map/reduce_sum | solution.py:117
  317.9 8.7 %gather_fusion = bf16[640,2048]{1,0:T(8,128)(2,1)} fusion(bf16[256,2048]{1,0:T(8,128)(2,1)} %get-tuple-element.21, s32[1024]{0:T(1024)S(1)} %pad_clamp_fusion.4), kind=kCustom, calls=%fused_computation.2 | custom fusion | bytes 5245440 | tf_op jit(solution)/shard_map/gather | solution.py:51
  326.6 5.1 gather.31
  331.7 3.8 broadcast_select_fusion.2
  335.6 14.1 %all-to-all-start = ((bf16[32,20,2048]{2,1,0:T(8,128)(2,1)}), bf16[32,20,2048]{2,1,0:T(8,128)(2,1)}, u32[]{:S(2)}, u32[]{:S(2)}) async-start(bf16[32,20,2048]{2,1,0:T(8,128)(2,1)} %broadcast_select_fusion.2), calls=%async_computation | async-start | bytes 6291456 | tf_op jit(solution)/shard_map/all_to_all | solution.py:174
  350.3 37.6 %all-to-all-done = bf16[32,20,2048]{2,1,0:T(8,128)(2,1)} async-done(((bf16[32,20,2048]{2,1,0:T(8,128)(2,1)}), bf16[32,20,2048]{2,1,0:T(8,128)(2,1)}, u32[]{:S(2)}, u32[]{:S(2)}) %all-to-all-start) | async-done | bytes 2621472 | tf_op jit(solution)/shard_map/all_to_all | solution.py:174
  387.9 5.2 reshape.451
  393.1 6.2 fusion.13
  399.3 9.6 %convolution_convert_fusion.4 = bf16[640,2048]{1,0:T(8,128)(2,1)} fusion(bf16[1,1,768,2048]{3,2,1,0:T(8,128)(2,1)} %param.19, f32[640,768]{1,0:T(8,128)} %fusion.13, bf16[640,2048]{1,0:T(8,128)(2,1)} %reshape.451, bf16[1,1,2048,768]{3,2,1,0:T(8,128)(2,1)S(1)} %copy-done), kind=kOutput, calls=%fused_computation.18 | convolution fusion | flops 4030791680 | bytes 13500416 | tf_op jit(solution)/shard_map/dot_general | solution.py:75
  408.9 5.1 reshape.452
  414.0 6.3 all-to-all-start.1
  422.2 4.6 gather_fusion.7
  427.2 6.5 fusion.15
  433.7 4.0 fusion.16
  437.8 4.1 fusion.17
  443.3 98.5 %psum.15 = f32[1,2048]{1,0:T(1,128)} all-reduce(f32[1,2048]{1,0:T(1,128)S(1)} %bitcast.153), channel_id=1, replica_groups=mesh['pipe'=4,'expert'=32] {'expert'}, use_global_device_ids=true, to_apply=%region_18.20 | all-reduce | flops 2048 | bytes 16384 | tf_op jit(solution)/shard_map/psum | solution.py:206
  541.7 5.2 reshape.453
  550.5 7.4 gather_fusion.1
  557.9 5.4 reshape.461
  563.3 8.9 %multiply_reduce_fusion.1 = f32[256,2048]{1,0:T(8,128)S(1)} fusion(f32[256,2,2048]{2,1,0:T(2,128)} %reshape.461, f32[256,2]{1,0:T(8,128)S(1)} %copy.50), kind=kLoop, calls=%fused_computation.13 | loop fusion | flops 1572864 | bytes 6293504 | tf_op jit(solution)/shard_map/reduce_sum | solution.py:66
  574.7 228.2 %all-reduce.4.cloned.1.call-done = f32[1,2048,32]{1,2,0:T(8,128)} async-done(((f32[1,2048,32]{1,2,0:T(8,128)}), f32[1,2048,32]{1,2,0:T(8,128)}) %all-reduce.4.cloned.1.call-update) | async-done | bytes 262160 | tf_op jit(solution)/shard_map/psum | solution.py:206
  (129 shorter events, 44.7 us)
Async XLA Ops:
  7.2 173.0 %copy-start = (bf16[1,1,2048,768]{3,2,1,0:T(8,128)(2,1)S(1)}, bf16[1,1,2048,768]{3,2,1,0:T(8,128)(2,1)}, u32[]{:S(2)}) copy-start(bf16[1,1,2048,768]{3,2,1,0:T(8,128)(2,1)} %param.18) | copy-start | bytes 9437188
  7.2 44.4 %collective-permute-start.1 = (bf16[1,256,2048]{2,1,0:T(8,128)(2,1)}, bf16[1,256,2048]{2,1,0:T(8,128)(2,1)}, u32[]{:S(2)}, u32[]{:S(2)}) collective-permute-start(bf16[1,256,2048]{2,1,0:T(8,128)(2,1)} %param.16), channel_id=1, source_target_pairs={{32,0},{64,32},{96,64},{0,96},{33,1},{65,33},{97,65},{1,97},{34,2}... | collective-permute-start | bytes 3145736 | tf_op jit(solution)/shard_map/ppermute | solution.py:12
  13.4 4.8 copy-start.8
  13.4 5.2 copy-start.10
  18.0 17.7 %copy-start.7 = (f32[1,2048]{1,0:T(1,128)S(1)}, f32[1,2048]{1,0:T(1,128)}, u32[]{:S(2)}) copy-start(f32[1,2048]{1,0:T(1,128)} %param.21) | copy-start | bytes 24580
  24.9 45.0 %all-to-all-start.2 = ((bf16[32,20,1]{1,2,0:T(2,128)(2,1)}), bf16[32,20,1]{1,2,0:T(2,128)(2,1)S(1)}, u32[]{:S(2)}, u32[]{:S(2)}) async-start(bf16[32,20,1]{1,2,0:T(2,128)(2,1)} %convert_element_type.225), calls=%async_computation.2 | async-start | bytes 32768 | tf_op jit(solution)/shard_map/all_to_all | solution.py:184
  120.7 47.0 %all-to-all-start.4 = ((bf16[32,20,2048]{2,1,0:T(8,128)(2,1)}), bf16[32,20,2048]{2,1,0:T(8,128)(2,1)}, u32[]{:S(2)}, u32[]{:S(2)}) async-start(bf16[32,20,2048]{2,1,0:T(8,128)(2,1)} %get-tuple-element.23), calls=%async_computation.4 | async-start | bytes 6291456 | tf_op jit(solution)/shard_map/all_to_all | solution.py:182
  172.9 5.0 copy-start.5
  172.9 5.0 copy-start.12
  177.9 2.3 copy-start.3
  196.8 20.6 %all-to-all-start.6 = ((bf16[32,20,1]{1,2,0:T(2,128)(2,1)}), bf16[32,20,1]{1,2,0:T(2,128)(2,1)S(1)}, u32[]{:S(2)}, u32[]{:S(2)}) async-start(bf16[32,20,1]{1,2,0:T(2,128)(2,1)} %convert_element_type.226), calls=%async_computation.6 | async-start | bytes 32768 | tf_op jit(solution)/shard_map/all_to_all | solution.py:191
  204.0 4.5 copy-start.14
  217.4 10.2 %copy-start.11 = (s32[1,256]{1,0:T(1,128)S(1)}, s32[1,256]{1,0:T(1,128)}, u32[]{:S(2)}) copy-start(s32[1,256]{1,0:T(1,128)} %param.24) | copy-start | bytes 3076
  217.4 10.4 %copy-start.9 = (s32[1,256,2]{1,2,0:T(2,128)S(1)}, s32[1,256,2]{1,2,0:T(2,128)}, u32[]{:S(2)}) copy-start(s32[1,256,2]{1,2,0:T(2,128)} %param.22) | copy-start | bytes 6148
  217.4 63.1 %all-to-all-start.5 = ((bf16[32,20,2048]{2,1,0:T(8,128)(2,1)}), bf16[32,20,2048]{2,1,0:T(8,128)(2,1)}, u32[]{:S(2)}, u32[]{:S(2)}) async-start(bf16[32,20,2048]{2,1,0:T(8,128)(2,1)} %reshape.456), calls=%async_computation.5 | async-start | bytes 6291456 | tf_op jit(solution)/shard_map/all_to_all | solution.py:190
  227.5 47.3 %collective-permute-start = (bf16[1,256,2048]{2,1,0:T(8,128)(2,1)}, bf16[1,256,2048]{2,1,0:T(8,128)(2,1)}, u32[]{:S(2)}, u32[]{:S(2)}) collective-permute-start(bf16[1,256,2048]{2,1,0:T(8,128)(2,1)} %param.14), channel_id=1, source_target_pairs={{96,0},{0,32},{32,64},{64,96},{97,1},{1,33},{33,65},{65,97},{98,2}... | collective-permute-start | bytes 3145736 | tf_op jit(solution)/shard_map/ppermute | solution.py:12
  302.1 8.5 %copy-start.6 = (bf16[1,2048,32]{1,2,0:T(8,128)(2,1)S(1)}, bf16[1,2048,32]{1,2,0:T(8,128)(2,1)}, u32[]{:S(2)}) copy-start(bf16[1,2048,32]{1,2,0:T(8,128)(2,1)} %param.20) | copy-start | bytes 393220
  310.6 3.6 copy-start.2
  335.6 52.3 %all-to-all-start = ((bf16[32,20,2048]{2,1,0:T(8,128)(2,1)}), bf16[32,20,2048]{2,1,0:T(8,128)(2,1)}, u32[]{:S(2)}, u32[]{:S(2)}) async-start(bf16[32,20,2048]{2,1,0:T(8,128)(2,1)} %broadcast_select_fusion.2), calls=%async_computation | async-start | bytes 6291456 | tf_op jit(solution)/shard_map/all_to_all | solution.py:174
  414.0 127.7 %all-to-all-start.1 = ((bf16[32,20,2048]{2,1,0:T(8,128)(2,1)}), bf16[32,20,2048]{2,1,0:T(8,128)(2,1)}, u32[]{:S(2)}, u32[]{:S(2)}) async-start(bf16[32,20,2048]{2,1,0:T(8,128)(2,1)} %reshape.452), calls=%async_computation.1 | async-start | bytes 6291456 | tf_op jit(solution)/shard_map/all_to_all | solution.py:179
  420.3 382.6 %all-reduce.4.cloned.1.call-start = ((), (), s32[]{:S(2)}) async-start(), calls=%async_computation.7 | async-start | bytes 524288 | tf_op jit(solution)/shard_map/psum | solution.py:206
  427.2 6.5 copy-start.4
  427.2 6.5 copy-start.15
  427.2 10.6 %slice-start = ((s8[5242880]{0:T(1024)(128)(4,1)}), s8[4194304]{0:T(1024)(128)(4,1)S(1)}, s32[]{:S(2)}) async-start(s8[5242880]{0:T(1024)(128)(4,1)} %bitcast.144), calls=%async_computation.8 | async-start | bytes 8388608
  433.7 4.1 slice-start.1
  433.7 4.1 copy-start.13
  437.8 4.1 copy-start.1
Sparse Core Ops, SparseCore 0:
  443.4 359.4 all-reduce.3
where the time goes:
time: 822 us; the launch traced here: 812 us
  waiting for transfers between devices  344 us (42%)
  blocking collectives  149 us (18%)
  local copies, waits for them, and re-layouts  140 us (17%)
  matrix products  64.6 us (8%)
  starting transfers between devices  54.8 us (7%)
  other arithmetic  44.7 us (5%)
  between operations  14.9 us (2%)
    psum x1, waiting for transfers between devices, per_device(): router_total, gain_total = lax.psum((router_part, dgain), 'expert')  228 us
    psum x1, blocking collectives, per_device(): router_total, gain_total = lax.psum((router_part, dgain), 'expert')  98.5 us
    all_to_all x1, blocking collectives, per_device(): lax.all_to_all(cot_rows, 'expert', split_axis=0, concat_axis=0, tiled=True)  50.8 us
    ppermute x2, waiting for transfers between devices, passed_along(): return lax.ppermute(block, axis, route)  45.4 us
    all_to_all x1, waiting for transfers between devices, per_device(): lax.all_to_all(fwd_rows, 'expert', split_axis=0, concat_axis=0, tiled=True)  37.6 us
    all_to_all x1, waiting for transfers between devices, per_device(): lax.all_to_all(rows, 'expert', split_axis=0, concat_axis=0, tiled=True)  32.4 us
    gather x4, local copies, waits for them, and re-layouts, prepare(): normed[token]  27.2 us
    gather x3, local copies, waits for them, and re-layouts, pick_rows(): return padded[slots].astype(jnp.float32)  18.4 us
  transfers between devices with their start and end apart: 9, of which 4 were waited for; matrix products, arithmetic and copies ran while one was open for 17% of the time, Pallas kernels for 0%

commit v1 on v0

v1 whole, which is shorter than its diff:
```python
import functools

import jax
import jax.numpy as jnp
from jax import lax
from jax.experimental import pallas as pl
from jax.experimental.pallas import tpu as pltpu
from jax.sharding import PartitionSpec as P

EPS = 1e-06
MESH = pl.DeviceIdType.MESH
BF = jnp.bfloat16
F32 = jnp.float32
E = 32
T = 256
D = 2048
FF = 768
R = 640
RA = 512
Q = 512


def iota(shape, dim):
    return lax.broadcasted_iota(jnp.int32, shape, dim)


def dot(a, b):
    return jnp.dot(a, b, preferred_element_type=F32)


def dot_nt(a, b):
    return lax.dot_general(a, b, (((1,), (1,)), ((), ())), preferred_element_type=F32)


def halves(a):
    high = a.astype(BF)
    return high, (a - high.astype(F32)).astype(BF)


def cols(i, width):
    return pl.ds(pl.multiple_of(i * width, width), width)


def body(
    nx, cot, gw, uw, dw, xp, router, gain, nroutes, proutes, nprio, pprio,
    fout, gin, ggrad, ugrad, dgrad, rgrad, gaing,
    wg, wu, wd, xin, dyin, rpad, normp, normf,
    sa, sb, sat, sbt, wahi, walo, wbhi, wblo, dlt, prow, perm, permt,
    sx, sxb, sy, syb, sf, sfb, rx, rxb, ry, ryb, rf, rfb,
    gbuf, ubuf, act, gpart, upart, actt, iacc, itile, irecv,
    od, ost, odb, of, ofb, qd, qdb, qf, qfb, dn,
    rps, rrecv, rsum, rall, gsend, grecv,
    wsem, psend, precv, xs, xr, ls, osem,
):
    me = lax.axis_index("expert")
    pipe = lax.axis_index("pipe")
    n_pipe = lax.axis_size("pipe")
    ahead, behind = lax.rem(pipe + 1, n_pipe), lax.rem(pipe + n_pipe - 1, n_pipe)
    mx, mz, my = me // 8, (me // 2) % 4, me % 2

    def peer_of(k):
        return ((mx + k // 8) % 4) * 8 + ((mz + (k // 2) % 4) % 4) * 2 + (my + k % 2) % 2

    loads = [
        pltpu.make_async_copy(src, dst, wsem.at[i])
        for i, (src, dst) in enumerate(((gw, wg), (uw, wu), (dw, wd)))
    ]
    for load in loads:
        load.start()

    barrier = pltpu.get_barrier_semaphore()

    @pl.loop(1, E)
    def _(k):
        pl.semaphore_signal(barrier, 1, device_id={"expert": peer_of(k)}, device_id_type=MESH)

    for other in (ahead, behind):
        pl.semaphore_signal(barrier, 1, device_id={"pipe": other}, device_id_type=MESH)
    pl.semaphore_wait(barrier, E + 1)

    pipes = [
        pltpu.make_async_remote_copy(
            cot, dyin, psend.at[0], precv.at[0], device_id={"pipe": behind}, device_id_type=MESH
        ),
        pltpu.make_async_remote_copy(
            nx, xin, psend.at[1], precv.at[1], device_id={"pipe": ahead}, device_id_type=MESH
        ),
    ]
    for copy in pipes:
        copy.start()

    def send(index, src, dst, rows):
        mine = pl.ds(pl.multiple_of(me * rows, rows), rows)

        @pl.loop(1, E)
        def _(k):
            to = peer_of(k)
            theirs = pl.ds(pl.multiple_of(to * rows, rows), rows)
            pltpu.make_async_remote_copy(
                src.at[theirs], dst.at[mine], xs.at[index], xr.at[index],
                device_id={"expert": to}, device_id_type=MESH,
            ).start()

        pltpu.make_async_copy(src.at[mine], dst.at[mine], ls.at[index]).start()

    def received(index, src, dst, rows):
        mine = pl.ds(pl.multiple_of(me * rows, rows), rows)
        others = pl.ds(0, (E - 1) * rows)
        pltpu.make_async_copy(src.at[others], dst.at[others], xr.at[index]).wait()
        pltpu.make_async_copy(src.at[mine], dst.at[mine], ls.at[index]).wait()

    def sent(index, src, rows):
        others = pl.ds(0, (E - 1) * rows)
        pltpu.make_async_copy(src.at[others], src.at[others], xs.at[index]).wait()

    rpad[...] = jnp.zeros_like(rpad)
    rpad[:, 0:E] = router[...]
    expand = (iota((RA, 128), 0) // 16 == iota((RA, 128), 1)).astype(F32).astype(BF)
    expandt = (iota((128, RA), 1) // 16 == iota((128, RA), 0)).astype(F32).astype(BF)

    def normalise(x, norm):
        @pl.loop(0, T // 64)
        def _(i):
            rows = cols(i, 64)
            v = x[rows, :].astype(F32)
            scale = lax.rsqrt(jnp.sum(v * v, axis=1, keepdims=True) * (1.0 / D) + EPS)
            norm[rows, :] = (v * scale * gain[...]).astype(BF)

    def picks(routes):
        e = iota((128, T), 0)
        return e == routes[0:1, :], e == routes[1:2, :]

    def gates(norm, first, second):
        logits = dot(norm[...], rpad[...]).T
        s0 = jax.nn.sigmoid(jnp.sum(jnp.where(first, logits, 0.0), axis=0, keepdims=True))
        s1 = jax.nn.sigmoid(jnp.sum(jnp.where(second, logits, 0.0), axis=0, keepdims=True))
        total = s0 + s1
        return s0, s1, s0 / total, s1 / total

    def ranks(first, second, prio):
        across = jnp.broadcast_to(prio[...].astype(F32), (T, T))
        before = jnp.where(across.T < across, 1.0, 0.0).astype(BF)
        chosen = jnp.where(first | second, 1.0, 0.0)
        count = dot(chosen.astype(BF), before)
        return jnp.where(first | second, count, -1.0)

    row16 = (iota((RA, T), 0) % 16).astype(F32)
    row4 = (iota((RA, T), 0) % 4).astype(F32) + 16.0
    col16 = (iota((T, RA), 1) % 16).astype(F32)
    col4 = (iota((T, RA), 1) % 4).astype(F32) + 16.0

    def fill(source, a, b, first_a, first_b):
        mask = (iota((RA, T), 0) % 16) // 4

        @pl.loop(0, 4)
        def _(q):
            part = cols(q, Q)
            a[:, part] = dot(first_a[...], source[:, part]).astype(BF)

        total = jnp.zeros((RA, Q), F32)
        picked = first_b[...].astype(F32)
        for q in range(4):
            own = jnp.where(mask == q, picked, 0.0).astype(BF)
            total = total + dot(own, source[:, q * Q : (q + 1) * Q])
        b[:, 0:Q] = total.astype(BF)

    normalise(xp, normp)
    first, second = picks(proutes)
    s0, s1, w0, w1 = gates(normp, first, second)
    prow[0:1, :] = s0
    prow[1:2, :] = s1
    prow[2:3, :] = w0
    prow[3:4, :] = w1
    rank = ranks(first, second, pprio)
    spread = dot(expand, rank.astype(BF))
    take_a = jnp.where(spread == row16, 1.0, 0.0)
    take_b = jnp.where(spread == row4, 1.0, 0.0)
    sa[...] = take_a.astype(BF)
    sb[...] = take_b.astype(BF)
    fill(normp, sx, sxb, sa, sb)
    send(0, sx, rx, 16)
    send(1, sxb, rxb, 16)

    weight = jnp.where(first, w0, 0.0) + jnp.where(second, w1, 0.0)
    spread_w = dot(expand, weight.astype(BF))
    wa = jnp.sum(take_a * spread_w, axis=1, keepdims=True)
    wb = jnp.sum(take_b * spread_w, axis=1, keepdims=True)
    lane = iota((RA, 128), 1)
    syb[:, Q : Q + 128] = jnp.where(lane < 64, wa, wb).astype(BF)
    spread_t = dot(rank.T.astype(BF), expandt)
    sat[...] = jnp.where(spread_t == col16, 1.0, 0.0).astype(BF)
    sbt[...] = jnp.where(spread_t == col4, 1.0, 0.0).astype(BF)
    i0, i1 = iota((RA, RA), 0), iota((RA, RA), 1)
    perm[...] = jnp.where(
        i1 == ((i0 % 128) // 4) * 16 + (i0 // 128) * 4 + i0 % 4, 1.0, 0.0
    ).astype(BF)
    permt[...] = jnp.where(
        i0 == ((i1 % 128) // 4) * 16 + (i1 // 128) * 4 + i1 % 4, 1.0, 0.0
    ).astype(BF)

    pipes[0].wait_recv()
    fill(dyin, sy, syb, sa, sb)
    send(2, sy, ry, 16)
    send(3, syb, ryb, 16)

    pipes[1].wait_recv()
    normalise(xin, normf)
    first, second = picks(nroutes)
    s0, s1, w0, w1 = gates(normf, first, second)
    rank = ranks(first, second, nprio)
    spread = dot(expand, rank.astype(BF))
    wahi[...] = jnp.where(spread == row16, 1.0, 0.0).astype(BF).T
    wbhi[...] = jnp.where(spread == row4, 1.0, 0.0).astype(BF).T
    walo[...] = jnp.zeros_like(walo)
    wblo[...] = jnp.zeros_like(wblo)
    od[0:RA, 0:T] = jnp.where(spread == row16, 1.0, 0.0).astype(BF)
    od[0:RA, T : 2 * T] = jnp.where(spread == row4, 1.0, 0.0).astype(BF)
    fill(normf, sf, sfb, od.at[0:RA, 0:T], od.at[0:RA, T : 2 * T])
    send(4, sf, rf, 16)
    send(5, sfb, rfb, 16)
    weight = jnp.where(first, w0, 0.0) + jnp.where(second, w1, 0.0)
    high, low = halves(weight.T)
    spread_t = dot(rank.T.astype(BF), expandt)
    spread_hi, spread_lo = dot(high, expandt), dot(low, expandt)
    wahi[...] = jnp.where(spread_t == col16, spread_hi, 0.0).astype(BF)
    walo[...] = jnp.where(spread_t == col16, spread_lo, 0.0).astype(BF)
    wbhi[...] = jnp.where(spread_t == col4, spread_hi, 0.0).astype(BF)
    wblo[...] = jnp.where(spread_t == col4, spread_lo, 0.0).astype(BF)

    def unpack(b, x):
        stacked = dot(perm[...], b[:, 0:Q]).astype(BF)
        for q in range(4):
            x[RA:R, q * Q : (q + 1) * Q] = stacked[q * 128 : (q + 1) * 128]

    received(0, sx, rx, 16)
    received(1, sxb, rxb, 16)
    unpack(rxb, rx)
    loads[0].wait()
    loads[1].wait()

    @pl.loop(0, FF // 256)
    def _(n):
        part = cols(n, 256)
        g = dot(rx[...], wg[:, part])
        u = dot(rx[...], wu[:, part])
        gbuf[:, part] = g
        ubuf[:, part] = u
        act[:, part] = (g * jax.nn.sigmoid(g) * u).astype(BF)

    received(2, sy, ry, 16)
    received(3, syb, ryb, 16)
    unpack(ryb, ry)
    loads[2].wait()
    iacc[...] = jnp.zeros_like(iacc)

    @pl.loop(0, 4)
    def _(q):
        part = cols(q, Q)
        result = dot(act[...], wd[:, part]).astype(BF).astype(F32)
        product = result * ry[:, part].astype(F32)
        total = product[:, 0:128]
        for i in range(1, 4):
            total = total + product[:, i * 128 : (i + 1) * 128]
        iacc[...] += total

    inner = jnp.sum(iacc[...], axis=1, keepdims=True).astype(BF).astype(F32)
    inner_b = jnp.broadcast_to(inner[RA:R], (128, 128)).astype(BF)
    placed_b = dot(permt[:, 0:128], inner_b)
    itile[...] = jnp.where(lane < 64, inner[0:RA], placed_b).astype(BF)
    send(6, itile, irecv, 16)

    scale_b = dot(perm[0:128, :], ryb[:, Q : Q + 128])[:, 64:65]
    scale_a = ryb[:, Q : Q + 1].astype(F32)

    @pl.loop(0, 4)
    def _(q):
        part = cols(q, Q)
        ry[0:RA, part] = (ry[0:RA, part].astype(F32) * scale_a).astype(BF)
        ry[RA:R, part] = (ry[RA:R, part].astype(F32) * scale_b).astype(BF)

    @pl.loop(0, FF // 256)
    def _(n):
        part = cols(n, 256)
        back = dot_nt(ry[...], wd[part, :])
        g = gbuf[:, part]
        sig = jax.nn.sigmoid(g)
        gpart[:, part] = (back * ubuf[:, part] * sig * (1.0 + g * (1.0 - sig))).astype(BF)
        upart[:, part] = (back * g * sig).astype(BF)

    def put(out, q, a, stack):
        a[:, cols(q, Q)] = out[0:RA]
        stack[cols(q, 128), :] = out[RA:R]

    @pl.loop(0, 4)
    def _(q):
        part = cols(q, Q)
        out = dot_nt(gpart[...], wg[part, :]) + dot_nt(upart[...], wu[part, :])
        put(out.astype(BF), q, od, ost)

    odb[...] = dot(permt[...], ost[...]).astype(BF)
    send(7, od, qd, 16)
    send(8, odb, qdb, 16)

    received(4, sf, rf, 16)
    received(5, sfb, rfb, 16)
    unpack(rfb, rf)

    @pl.loop(0, FF // 256)
    def _(n):
        part = cols(n, 256)
        g = dot(rf[...], wg[:, part])
        u = dot(rf[...], wu[:, part])
        gbuf[:, part] = g * jax.nn.sigmoid(g) * u

    actf = gbuf[...].astype(BF)

    @pl.loop(0, 4)
    def _(q):
        put(dot(actf, wd[:, cols(q, Q)]).astype(BF), q, of, ost)

    ofb[...] = dot(permt[...], ost[...]).astype(BF)
    send(9, of, qf, 16)
    send(10, ofb, qfb, 16)

    received(6, itile, irecv, 16)
    first, second = picks(proutes)
    mixed = (
        sa[...].astype(F32) * irecv[:, 0:1].astype(F32)
        + sb[...].astype(F32) * irecv[:, 64:65].astype(F32)
    )
    per_expert = dot(expandt, mixed.astype(BF))
    d0 = jnp.sum(jnp.where(first, per_expert, 0.0), axis=0, keepdims=True)
    d1 = jnp.sum(jnp.where(second, per_expert, 0.0), axis=0, keepdims=True)
    s0, s1, w0, w1 = prow[0:1, :], prow[1:2, :], prow[2:3, :], prow[3:4, :]
    shared = w0 * w1 * (d0 - d1)
    dlogits = jnp.where(first, shared * (1.0 - s0), 0.0) - jnp.where(
        second, shared * (1.0 - s1), 0.0
    )
    dlt[...] = dlogits
    high, low = halves(dlogits[0:E])
    both = jnp.concatenate([high, low], axis=0)
    for q in range(4):
        terms = dot(both, normp[:, q * Q : (q + 1) * Q])
        rps[:, q * Q : (q + 1) * Q] = terms[0:E] + terms[E : 2 * E]

    def tile_of(ref, owner):
        return ref.at[
            pl.ds(pl.multiple_of((owner // 8) * 8, 8), 8),
            pl.ds(pl.multiple_of((owner % 8) * 256, 256), 256),
        ]

    mine8 = pl.ds(pl.multiple_of(me * 8, 8), 8)

    @pl.loop(1, E)
    def _(k):
        to = peer_of(k)
        pltpu.make_async_remote_copy(
            tile_of(rps, to), rrecv.at[mine8], xs.at[11], xr.at[11],
            device_id={"expert": to}, device_id_type=MESH,
        ).start()

    pltpu.make_async_copy(tile_of(rps, me), rrecv.at[mine8], ls.at[11]).start()

    actt[...] = act[...].T

    @pl.loop(0, 4)
    def _(q):
        part = cols(q, Q)
        wd[:, part] = dot(actt[...], ry[:, part]).astype(BF)

    stores = [
        pltpu.make_async_copy(src, dst, osem.at[i])
        for i, (src, dst) in enumerate(((wg, ggrad), (wu, ugrad), (wd, dgrad)))
    ]
    stores[2].start()

    @pl.loop(0, 4)
    def _(q):
        part = cols(q, Q)
        turned = rx[:, part].T
        wg[part, :] = dot(turned, gpart[...]).astype(BF)
        wu[part, :] = dot(turned, upart[...]).astype(BF)

    stores[0].start()
    stores[1].start()

    others8 = pl.ds(0, (E - 1) * 8)
    pltpu.make_async_copy(rrecv.at[others8], rrecv.at[others8], xr.at[11]).wait()
    pltpu.make_async_copy(tile_of(rps, me), rrecv.at[mine8], ls.at[11]).wait()
    total = rrecv[0:8, :]
    for i in range(1, E):
        total = total + rrecv[i * 8 : (i + 1) * 8, :]
    rsum[...] = total

    @pl.loop(1, E)
    def _(k):
        pltpu.make_async_remote_copy(
            rsum, tile_of(rall, me), xs.at[12], xr.at[12],
            device_id={"expert": peer_of(k)}, device_id_type=MESH,
        ).start()

    pltpu.make_async_copy(rsum, tile_of(rall, me), ls.at[12]).start()

    received(7, od, qd, 16)
    received(8, odb, qdb, 16)
    dl_high, dl_low = halves(dlt[...].T)
    colq = (iota((T, RA), 1) % 16) // 4

    for q in range(4):
        part = slice(q * Q, (q + 1) * Q)
        own = jnp.where(colq == q, sbt[...].astype(F32), 0.0).astype(BF)
        total = dot(sat[...], qd[:, part]) + dot(own, qdb[...])
        total = total + dot_nt(dl_high, rpad[part, :]) + dot_nt(dl_low, rpad[part, :])
        dn[:, part] = total

    iacc_g = jnp.zeros((1, D), F32)

    def back_norm(i, acc):
        rows = cols(i, 64)
        v = xp[rows, :].astype(F32)
        scale = lax.rsqrt(jnp.sum(v * v, axis=1, keepdims=True) * (1.0 / D) + EPS)
        d = dn[rows, :]
        vs = v * scale
        h = d * gain[...]
        mean = jnp.sum(h * vs, axis=1, keepdims=True) * (1.0 / D)
        gin[rows, :] = (dyin[rows, :].astype(F32) + scale * (h - vs * mean)).astype(BF)
        return acc + jnp.sum(d * vs, axis=0, keepdims=True)

    acc = lax.fori_loop(0, T // 64, back_norm, iacc_g)
    for i in range(16):
        gsend[i : i + 1, :] = acc[:, i * 128 : (i + 1) * 128]
    mine = pl.ds(pl.multiple_of(me * 16, 16), 16)

    @pl.loop(1, E)
    def _(k):
        pltpu.make_async_remote_copy(
            gsend, grecv.at[mine], xs.at[13], xr.at[13],
            device_id={"expert": peer_of(k)}, device_id_type=MESH,
        ).start()

    pltpu.make_async_copy(gsend, grecv.at[mine], ls.at[13]).start()

    received(9, of, qf, 16)
    received(10, ofb, qfb, 16)
    for q in range(4):
        part = slice(q * Q, (q + 1) * Q)
        total = dot(wahi[...], qf[:, part]) + dot(walo[...], qf[:, part])
        for w in (wbhi, wblo):
            own = jnp.where(colq == q, w[...].astype(F32), 0.0).astype(BF)
            total = total + dot(own, qfb[...])
        fout[:, part] = (xin[:, part].astype(F32) + total).astype(BF)

    others16 = pl.ds(0, (E - 1) * 16)
    pltpu.make_async_copy(grecv.at[others16], grecv.at[others16], xr.at[13]).wait()
    pltpu.make_async_copy(gsend, grecv.at[mine], ls.at[13]).wait()
    total = grecv[0:16, :]
    for i in range(1, E):
        total = total + grecv[i * 16 : (i + 1) * 16, :]
    gaing[...] = total

    pltpu.make_async_copy(rrecv.at[others8], rrecv.at[others8], xr.at[12]).wait()
    pltpu.make_async_copy(rsum, tile_of(rall, me), ls.at[12]).wait()
    rgrad[...] = rall[...]

    for copy in pipes:
        copy.wait_send()
    for index, src in (
        (0, sx), (1, sxb), (2, sy), (3, syb), (4, sf), (5, sfb),
        (6, itile), (7, od), (8, odb), (9, of), (10, ofb), (13, grecv),
    ):
        sent(index, src, 16)
    for index in (11, 12):
        sent(index, rrecv, 8)
    for store in stores:
        store.wait()


def per_device(
    next_input, prev_input, next_cot, gate_weight, up_weight, down_weight,
    router, gain, next_routes, prev_routes, next_priority, prev_priority,
):
    anywhere = pl.BlockSpec(memory_space=pl.ANY)
    near = pl.BlockSpec(memory_space=pltpu.VMEM)
    vm = pltpu.VMEM
    grads = [jax.ShapeDtypeStruct(s, BF) for s in ((D, FF), (D, FF), (FF, D))]
    out = pl.pallas_call(
        body,
        name="slot",
        out_shape=[
            jax.ShapeDtypeStruct((T, D), BF),
            jax.ShapeDtypeStruct((T, D), BF),
            *grads,
            jax.ShapeDtypeStruct((E, D), F32),
            jax.ShapeDtypeStruct((16, 128), F32),
        ],
        in_specs=[anywhere] * 5 + [near] * 7,
        out_specs=[near, near, anywhere, anywhere, anywhere, near, near],
        scratch_shapes=[
            vm((D, FF), BF), vm((D, FF), BF), vm((FF, D), BF),
            vm((T, D), BF), vm((T, D), BF), vm((D, 128), BF),
            vm((T, D), BF), vm((T, D), BF),
            vm((RA, T), BF), vm((RA, T), BF), vm((T, RA), BF), vm((T, RA), BF),
            vm((T, RA), BF), vm((T, RA), BF), vm((T, RA), BF), vm((T, RA), BF),
            vm((128, T), F32), vm((8, T), F32),
            vm((RA, RA), BF), vm((RA, RA), BF),
            vm((RA, D), BF), vm((RA, Q), BF),
            vm((RA, D), BF), vm((RA, Q + 128), BF),
            vm((RA, D), BF), vm((RA, Q), BF),
            vm((R, D), BF), vm((RA, Q), BF),
            vm((R, D), BF), vm((RA, Q + 128), BF),
            vm((R, D), BF), vm((RA, Q), BF),
            vm((R, FF), F32), vm((R, FF), F32),
            vm((R, FF), BF), vm((R, FF), BF), vm((R, FF), BF),
            vm((FF, R), BF), vm((R, 128), F32),
            vm((RA, 128), BF), vm((RA, 128), BF),
            vm((RA, D), BF), vm((RA, Q), BF), vm((RA, Q), BF),
            vm((RA, D), BF), vm((RA, Q), BF),
            vm((RA, D), BF), vm((RA, Q), BF),
            vm((RA, D), BF), vm((RA, Q), BF),
            vm((T, D), F32),
            vm((E, D), F32), vm((256, 256), F32), vm((8, 256), F32), vm((E, D), F32),
            vm((16, 128), F32), vm((RA, 128), F32),
            pltpu.SemaphoreType.DMA((3,)),
            pltpu.SemaphoreType.DMA((2,)), pltpu.SemaphoreType.DMA((2,)),
            pltpu.SemaphoreType.DMA((14,)), pltpu.SemaphoreType.DMA((14,)),
            pltpu.SemaphoreType.DMA((14,)), pltpu.SemaphoreType.DMA((3,)),
        ],
        compiler_params=pltpu.CompilerParams(
            collective_id=0, has_side_effects=True, vmem_limit_bytes=67_000_000
        ),
    )(
        next_input[0], next_cot[0], gate_weight[0, 0], up_weight[0, 0], down_weight[0, 0],
        prev_input[0], router[0], gain, next_routes[0].T, prev_routes[0].T,
        next_priority, prev_priority,
    )
    fout, gin, gg, ug, dg, rg, gaing = out
    return (
        fout[None], gin[None], gg[None, None], ug[None, None], dg[None, None],
        rg.T[None], gaing.reshape(1, D),
    )


def solution(mesh):
    tokens = P("pipe", "expert", None)
    experts = P("pipe", "expert", None, None)
    return jax.shard_map(
        per_device,
        mesh=mesh,
        in_specs=(
            tokens, tokens, tokens, experts, experts, experts,
            P("pipe", None, None), P("pipe", None), tokens, tokens,
            P("pipe", "expert"), P("pipe", "expert"),
        ),
        out_specs=(
            tokens, tokens, experts, experts, experts,
            P("pipe", None, None), P("pipe", None),
        ),
        check_vma=False,
    )
```

time: 822 us -> 230 us (0.28); the launches traced: 812 us -> 230 us
  waiting for transfers between devices: 344 us -> 0 us
  Pallas kernels: 0 us -> 214 us
  blocking collectives: 149 us -> 0 us
  local copies, waits for them, and re-layouts: 140 us -> 15.7 us
  matrix products: 64.6 us -> 0 us
  starting transfers between devices: 54.8 us -> 0 us
  other arithmetic: 44.7 us -> 0 us
  between operations: 14.9 us -> 0.66 us
    psum x1 -> x0, waiting for transfers between devices: 228 us -> none  [per_device(): router_total, gain_total = lax.psum((router_part, dgain), 'expert')]
    pallas_call x0 -> x1, Pallas kernels: none -> 214 us  [per_device(): pl.pallas_call(body, name='slot', out_shape=[jax.ShapeDtypeStruct((T, D),...]
    psum x1 -> x0, blocking collectives: 98.5 us -> none  [per_device(): router_total, gain_total = lax.psum((router_part, dgain), 'expert')]
    gather x20 -> x0, local copies, waits for them, and re-layouts: 73.4 us -> none  [the longest x4 27.2 us: prepare(): normed[token]]
    all_to_all x6 -> x0, waiting for transfers between devices: 70 us -> none  [the longest x1 37.6 us: per_device(): lax.all_to_all(fwd_rows, 'expert', split_axis=0, concat_axis=0, tiled=True)]
    dot_general x15 -> x0, matrix products: 64.6 us -> none  [the longest x1 9.63 us: expert_forward(): jnp.dot(active, down_w[0], preferred_element_type=jnp.float32)]
    all_to_all x6 -> x0, starting transfers between devices: 53.5 us -> none  [the longest x1 14.1 us: per_device(): lax.all_to_all(fwd_rows, 'expert', split_axis=0, concat_axis=0, tiled=True)]
    all_to_all x1 -> x0, blocking collectives: 50.8 us -> none  [per_device(): lax.all_to_all(cot_rows, 'expert', split_axis=0, concat_axis=0, tiled=True)]
  transfers between devices with their start and end apart: 9 -> 0, of which waited for: 4 -> 0; matrix products, arithmetic and copies ran while one was open for 17% -> 0% of each run, Pallas kernels for 0% -> 0%
where the time goes in v1:
time: 230 us
  Pallas kernels  214 us (93%)
  local copies, waits for them, and re-layouts  15.7 us (7%)
    pallas_call x1, Pallas kernels, per_device(): pl.pallas_call(body, name='slot', out_shape=[jax.ShapeDtypeStruct((T, D),...  214 us
    unnamed x18, local copies, waits for them, and re-layouts  15.7 us

profile of v1, /device:TPU:0, one launch (start us, length us, event | category | flops | bytes accessed | tf_op | source)
XLA Modules:
  0.0 229.9 jit_solution(16062668373883720594)
XLA Ops:
  0.6 1.9 copy.19
  2.5 213.6 %slot.1 = (bf16[256,2048]{1,0:T(8,128)(2,1)}, bf16[256,2048]{1,0:T(8,128)(2,1)}, bf16[2048,768]{1,0:T(8,128)(2,1)}, bf16[2048,768]{1,0:T(8,128)(2,1)}, bf16[768,...) custom-call(bf16[256,2048]{1,0:T(8,128)(2,1)} %bitcast.29, bf16[256,2048]{1,0:T(8,128)(2,1)} %bitcast.30, ...), custom_call_target="tpu_custom_call" | custom-call | tf_op jit(solution)/shard_map/slot/pallas_call | solution.py:486
  216.1 0.0 copy-start.2
  216.2 2.5 %copy.27 = bf16[1,256,2048]{2,1,0:T(8,128)(2,1)} copy(bf16[1,256,2048]{2,1,0:T(8,128)(2,1)} %bitcast.33) | data formatting | bytes 2097152
  218.6 2.3 %copy.28 = bf16[1,256,2048]{2,1,0:T(8,128)(2,1)} copy(bf16[1,256,2048]{2,1,0:T(8,128)(2,1)} %bitcast.32) | data formatting | bytes 2097152
  220.9 0.0 copy-done.2
  220.9 0.0 copy-start.1
  220.9 1.7 copy.29
  222.6 1.4 copy-done.1
  223.9 0.0 copy-start
  223.9 1.7 copy.30
  225.6 1.4 copy-done
  227.0 0.0 copy-start.3
  227.0 0.0 copy-start.4
  227.0 1.7 copy.31
  228.6 0.0 copy-done.3
  228.6 0.7 copy.32
  229.3 0.0 copy-done.4
  229.3 0.6 copy.33
Async XLA Ops:
  216.1 4.8 %copy-start.2 = (bf16[2048,768]{1,0:T(8,128)(2,1)S(1)}, bf16[2048,768]{1,0:T(8,128)(2,1)}, u32[]{:S(2)}) copy-start(bf16[2048,768]{1,0:T(8,128)(2,1)} %get-tuple-element.16) | copy-start | bytes 9437188
  220.9 3.0 %copy-start.1 = (bf16[2048,768]{1,0:T(8,128)(2,1)S(1)}, bf16[2048,768]{1,0:T(8,128)(2,1)}, u32[]{:S(2)}) copy-start(bf16[2048,768]{1,0:T(8,128)(2,1)} %get-tuple-element.17) | copy-start | bytes 9437188
  223.9 3.0 %copy-start = (bf16[768,2048]{1,0:T(8,128)(2,1)S(1)}, bf16[768,2048]{1,0:T(8,128)(2,1)}, u32[]{:S(2)}) copy-start(bf16[768,2048]{1,0:T(8,128)(2,1)} %get-tuple-element.18) | copy-start | bytes 9437188
  227.0 1.7 copy-start.3
  227.0 2.4 %copy-start.4 = (f32[16,128]{1,0:T(8,128)S(1)}, f32[16,128]{1,0:T(8,128)}, u32[]{:S(2)}) copy-start(f32[16,128]{1,0:T(8,128)} %get-tuple-element.20) | copy-start | bytes 24580
